TPU v7x, 1024 devices: a whole 8x8x8 slice. The times are simulated.
1024 devices in a mesh: dp: 64 (over x, z), ctx: 16 (over y, core).
Axes of the slice: x: 8, y: 8, z: 8, core: 2. Of those that a mesh axis runs over, the one named last changes fastest.
Arguments:
- queries: bfloat16 [64, 16, 2, 64, 2048], P('dp', 'ctx'), may hold values from -6 to 6
- keys: bfloat16 [64, 16, 2, 64, 512], P('dp', 'ctx'), may hold values from -6 to 6
- values: bfloat16 [64, 16, 2, 64, 512], P('dp', 'ctx'), may hold values from -6 to 6
- out_grad: bfloat16 [64, 16, 2, 64, 2048], P('dp', 'ctx'), may hold values from -6 to 6
- layer_input: bfloat16 [64, 16, 2, 64, 4096], P('dp', 'ctx'), may hold values from -6 to 6
- doc_lengths: int32 [64, 64], P('dp'), may hold values from 1 to 64, as said below
Outputs:
- query_grad: bfloat16 [64, 16, 2, 64, 2048], P('dp', 'ctx')
- key_grad: bfloat16 [64, 16, 2, 64, 512], P('dp', 'ctx')
- value_grad: bfloat16 [64, 16, 2, 64, 512], P('dp', 'ctx')
- weight_grad: float32 [4096, 512], P('ctx', 'dp')
Inputs may be any that keep to these rules, and one draw needn't show every extreme that they name: `doc_lengths`: each sequence is 64 documents laid end to end that fill its 2048 tokens; no document is longer than 64 tokens, and one of each sequence has exactly 64.
All inputs are finite; a program needn't handle non-finite values.
Results may differ from a plain program's by a relative error of at most 0.03.
Values may be sent and summed in bfloat16 or wider, within the bound.
No kernel may reach another device: no remote copies, remote signals or barrier semaphores. Data moves between devices by JAX's collectives and lax.ppermute only.
A program may use at most 32 MiB of HBM per device.

v0:
```python
import math

import jax
import jax.numpy as jnp
from jax import lax
from jax.sharding import PartitionSpec as P

HD = 128


def from_behind(value, axis, steps):
    count = lax.axis_size(axis)
    first, last = (max(0, -steps), min(count, count - steps))
    return lax.ppermute(value, axis, [(source, source + steps) for source in range(first, last)])


def doc_index(starts, positions):
    return jnp.sum((starts <= positions[..., None]).astype(jnp.int32), axis=-1) - 1


def attend(query_rows, key_block, value_block, grad_rows, query_pos, key_pos, starts):
    blocks, rows, query_width = query_rows.shape
    columns = key_block.shape[1]
    kv_heads = key_block.shape[2] // HD
    groups = query_width // HD // kv_heads
    inverse_root = 1.0 / math.sqrt(HD)
    query_heads = query_rows.reshape(blocks, rows, kv_heads, groups, HD)
    grad_heads = grad_rows.reshape(blocks, rows, kv_heads, groups, HD)
    key_heads = key_block.reshape(blocks, columns, kv_heads, HD)
    value_heads = value_block.reshape(blocks, columns, kv_heads, HD)
    query_doc = doc_index(starts, query_pos)
    key_doc = doc_index(starts, key_pos)
    allowed = (
        (query_doc[:, :, None] == key_doc[:, None, :])
        & (key_pos[:, None, :] <= query_pos[:, :, None])
        & (key_pos[:, None, :] >= 0)
    )
    scores = (
        jnp.einsum("bqngd,bknd->bngqk", query_heads, key_heads, preferred_element_type=jnp.float32)
        * inverse_root
    )
    scores = jnp.where(allowed[:, None, None], scores, -1e30)
    top_score = jnp.max(scores, axis=-1, keepdims=True)
    log_total = top_score + jnp.log(jnp.sum(jnp.exp(scores - top_score), axis=-1, keepdims=True))
    probs = jnp.exp(scores - log_total)
    probs_low = probs.astype(jnp.bfloat16)
    attn_out = jnp.einsum(
        "bngqk,bknd->bqngd", probs_low, value_heads, preferred_element_type=jnp.float32
    ).astype(jnp.bfloat16)
    delta = jnp.sum(grad_heads.astype(jnp.float32) * attn_out.astype(jnp.float32), axis=-1)
    dprob = jnp.einsum(
        "bqngd,bknd->bngqk", grad_heads, value_heads, preferred_element_type=jnp.float32
    )
    dscore = (probs * (dprob - jnp.transpose(delta, (0, 2, 3, 1))[..., None])).astype(jnp.bfloat16)
    query_grad = (
        jnp.einsum("bngqk,bknd->bqngd", dscore, key_heads, preferred_element_type=jnp.float32)
        * inverse_root
    ).astype(jnp.bfloat16)
    key_terms = (
        jnp.einsum("bngqk,bqngd->bknd", dscore, query_heads, preferred_element_type=jnp.float32)
        * inverse_root
    )
    value_terms = jnp.einsum(
        "bngqk,bqngd->bknd", probs_low, grad_heads, preferred_element_type=jnp.float32
    )
    return (
        query_grad.reshape(blocks, rows, query_width),
        key_terms.reshape(blocks, columns, kv_heads * HD),
        value_terms.reshape(blocks, columns, kv_heads * HD),
    )


def body(queries, keys, values, out_grad, layer_input, doc_lengths):
    span_rows = queries.shape[3]
    query_rows = queries[0, 0]
    key_rows = keys[0, 0]
    value_rows = values[0, 0]
    grad_rows = out_grad[0, 0]
    lengths = doc_lengths[0]
    starts = jnp.cumsum(lengths) - lengths
    device_place = lax.axis_index("ctx")
    ctx_count = lax.axis_size("ctx")
    offsets = jnp.arange(span_rows, dtype=jnp.int32)
    lower_pos = device_place * span_rows + offsets
    upper_pos = (2 * ctx_count - 1 - device_place) * span_rows + offsets
    at_fold = device_place == ctx_count - 1
    arrived = []
    for direction in (1, -1):
        arrived.append(from_behind((key_rows, value_rows), "ctx", direction))
    below_keys = arrived[0][0][0]
    below_values = arrived[0][1][0]
    above_keys = arrived[1][0][1]
    above_values = arrived[1][1][1]
    upper_prev_keys = jnp.where(at_fold, key_rows[0], above_keys)
    upper_prev_values = jnp.where(at_fold, value_rows[0], above_values)
    key_block = jnp.stack(
        [
            jnp.concatenate([below_keys, key_rows[0]], axis=0),
            jnp.concatenate([upper_prev_keys, key_rows[1]], axis=0),
        ]
    )
    value_block = jnp.stack(
        [
            jnp.concatenate([below_values, value_rows[0]], axis=0),
            jnp.concatenate([upper_prev_values, value_rows[1]], axis=0),
        ]
    )
    query_pos = jnp.stack([lower_pos, upper_pos])
    key_pos = jnp.stack(
        [
            jnp.concatenate([lower_pos - span_rows, lower_pos]),
            jnp.concatenate([upper_pos - span_rows, upper_pos]),
        ]
    )
    query_grad, key_terms, value_terms = attend(
        query_rows, key_block, value_block, grad_rows, query_pos, key_pos, starts
    )
    lower_keys = key_terms[0, span_rows:] + jnp.where(at_fold, key_terms[1, :span_rows], 0.0)
    lower_values = value_terms[0, span_rows:] + jnp.where(at_fold, value_terms[1, :span_rows], 0.0)
    upper_keys = key_terms[1, span_rows:]
    upper_values = value_terms[1, span_rows:]
    down_keys = key_terms[0, :span_rows]
    down_values = value_terms[0, :span_rows]
    up_keys = jnp.where(at_fold, 0.0, key_terms[1, :span_rows])
    up_values = jnp.where(at_fold, 0.0, value_terms[1, :span_rows])
    blank = jnp.zeros_like(down_keys)
    key_total = jnp.stack([lower_keys, upper_keys])
    value_total = jnp.stack([lower_values, upper_values])
    for direction, sent_keys, sent_values in (
        (-1, jnp.stack([down_keys, blank]), jnp.stack([down_values, blank])),
        (1, jnp.stack([blank, up_keys]), jnp.stack([blank, up_values])),
    ):
        came_keys, came_values = (
            from_behind(sent_keys.astype(jnp.bfloat16), "ctx", direction).astype(sent_keys.dtype),
            from_behind(sent_values.astype(jnp.bfloat16), "ctx", direction).astype(
                sent_values.dtype
            ),
        )
        key_total = key_total + came_keys
        value_total = value_total + came_values
    key_grad = key_total.astype(jnp.bfloat16)
    value_grad = value_total.astype(jnp.bfloat16)
    input_rows = layer_input[0, 0].reshape(2 * span_rows, layer_input.shape[4])
    grad_values = value_grad.reshape(2 * span_rows, value_grad.shape[2])
    row_block = lax.psum_scatter(
        lax.dot_general(
            input_rows, grad_values, (((0,), (0,)), ((), ())), preferred_element_type=jnp.float32
        ).astype(jnp.bfloat16),
        "ctx",
        scatter_dimension=0,
        tiled=True,
    ).astype(jnp.float32)
    weight_grad = lax.psum_scatter(row_block, "dp", scatter_dimension=1, tiled=True) / jnp.float32(
        lax.axis_size("dp")
    )
    return (query_grad[None, None], key_grad[None, None], value_grad[None, None], weight_grad)


def solution(mesh):
    in_specs = (
        P("dp", "ctx", None, None, None),
        P("dp", "ctx", None, None, None),
        P("dp", "ctx", None, None, None),
        P("dp", "ctx", None, None, None),
        P("dp", "ctx", None, None, None),
        P("dp", None),
    )
    out_specs = (
        P("dp", "ctx", None, None, None),
        P("dp", "ctx", None, None, None),
        P("dp", "ctx", None, None, None),
        P("ctx", "dp"),
    )
    return jax.shard_map(body, mesh=mesh, in_specs=in_specs, out_specs=out_specs, check_vma=False)
```

profile of v0, /device:TPU:8, one launch (start us, length us, event | category | flops | bytes accessed | tf_op | source)
XLA Modules:
  0.0 410.7 jit_solution(14432248718549253991)
XLA Ops:
  7.2 1.4 collective-permute-start.1
  8.7 3.0 collective-permute-start
  11.7 0.9 fusion.33
  12.8 1.4 reshape_squeeze.9
  14.3 0.7 copy.76
  16.2 1.4 reshape_squeeze.10
  19.1 0.9 fusion.16
  20.0 1.0 fusion.30
  21.7 1.7 copy.106
  23.4 1.7 copy.104
  25.9 3.9 collective-permute-start.7
  29.8 1.0 copy.107
  30.8 1.3 collective-permute-start.6
  32.1 0.9 select_add_fusion
  33.1 1.0 collective-permute-done.6
  34.1 1.0 fusion.22
  35.1 3.2 fusion
  38.4 1.3 collective-permute-start.3
  39.7 6.1 %collective-permute-start.2 = (bf16[2,64,512]{2,1,0:T(8,128)(2,1)S(1)}, bf16[2,64,512]{2,1,0:T(8,128)(2,1)}, u32[]{:S(2)}, u32[]{:S(2)}) collective-permute-start(bf16[2,64,512]{2,1,0:T(8,128)(2,1)S(1)} %bitcast.115), channel_id=1, source_target_pairs={{0,1},{1,2},{2,3},{3,4},{4,5},{5,6},{6,7},{7,8},{8,9},{9,10},{10,1... | collective-permute-start | bytes 393224 | tf_op jit(solution)/shard_map/ppermute | solution.py:14
  46.5 1.3 dynamic-slice
  48.5 0.9 copy_bitcast_fusion
  49.4 0.9 fusion.34
  50.2 1.5 fusion.10
  51.7 1.5 fusion.5
  53.2 0.8 copy-done.2
  54.7 1.2 broadcast_in_dim_reshape.3
  55.9 1.4 fusion.12
  57.7 3.0 collective-permute-start.5
  60.8 1.3 collective-permute-start.4
  62.4 2.9 collective-permute-done.4
  66.0 54.7 %reduce-scatter.2.cloned.1.call-done = bf16[256,512]{0,1:T(8,128)(2,1)} async-done(((bf16[4096,512]{0,1:T(8,128)(2,1)}), bf16[256,512]{0,1:T(8,128)(2,1)}) %reduce-scatter.2.cloned.1.call-update) | async-done | bytes 262160 | tf_op jit(solution)/shard_map/reduce_scatter | solution.py:145
  120.7 282.5 %all-reduce.6 = f32[256,512]{0,1:T(8,128)S(1)} all-reduce(bf16[256,512]{0,1:T(8,128)(2,1)} %reduce-scatter.2.cloned.1.call-done), channel_id=3, replica_groups=mesh['dp'=64,'ctx'=16] {'dp'}, use_global_device_ids=true, to_apply=%region_7.8.clone | all-reduce | flops 131072 | bytes 786432
  (78 shorter events, 7.8 us)
Async XLA Ops:
  7.2 27.9 %copy-start = (bf16[1,1,2,64,4096]{4,3,2,1,0:T(8,128)(2,1)S(1)}, bf16[1,1,2,64,4096]{4,3,2,1,0:T(8,128)(2,1)}, u32[]{:S(2)}) copy-start(bf16[1,1,2,64,4096]{4,3,2,1,0:T(8,128)(2,1)} %param.10) | copy-start | bytes 3145732
  7.2 113.5 %reduce-scatter.2.cloned.1.call-start = ((), (), s32[]{:S(2)}) async-start(), calls=%async_computation.1 | async-start | bytes 4456448 | tf_op jit(solution)/shard_map/reduce_scatter | solution.py:145
  7.2 10.6 %collective-permute-start.1 = (bf16[2,64,512]{2,1,0:T(8,128)(2,1)}, bf16[2,64,512]{2,1,0:T(8,128)(2,1)S(1)}, u32[]{:S(2)}, u32[]{:S(2)}) collective-permute-start(bf16[2,64,512]{2,1,0:T(8,128)(2,1)} %bitcast.112), channel_id=1, source_target_pairs={{1,0},{2,1},{3,2},{4,3},{5,4},{6,5},{7,6},{8,7},{9,8},{10,9},{11,1... | collective-permute-start | bytes 393224 | tf_op jit(solution)/shard_map/ppermute | solution.py:14
  8.7 9.1 %collective-permute-start = (bf16[2,64,512]{2,1,0:T(8,128)(2,1)}, bf16[2,64,512]{2,1,0:T(8,128)(2,1)S(1)}, u32[]{:S(2)}, u32[]{:S(2)}) collective-permute-start(bf16[2,64,512]{2,1,0:T(8,128)(2,1)} %bitcast.113), channel_id=1, source_target_pairs={{0,1},{1,2},{2,3},{3,4},{4,5},{5,6},{6,7},{7,8},{8,9},{9,10},{10,1... | collective-permute-start | bytes 393224 | tf_op jit(solution)/shard_map/ppermute | solution.py:14
  14.3 4.1 %copy-start.4 = (bf16[1,64,4,128]{3,1,2,0:T(8,128)(2,1)}, bf16[1,64,4,128]{3,1,2,0:T(8,128)(2,1)S(1)}, u32[]{:S(2)}) copy-start(bf16[1,64,4,128]{3,1,2,0:T(8,128)(2,1)S(1)} %copy.75) | copy-start | bytes 196612
  17.8 1.3 copy-start.6
  17.8 1.3 copy-start.8
  17.8 1.3 copy-start.10
  25.9 7.1 %collective-permute-start.7 = (bf16[2,64,512]{2,1,0:T(8,128)(2,1)}, bf16[2,64,512]{2,1,0:T(8,128)(2,1)}, u32[]{:S(2)}, u32[]{:S(2)}) collective-permute-start(bf16[2,64,512]{2,1,0:T(8,128)(2,1)} %stack.57), channel_id=1, source_target_pairs={{0,1},{1,2},{2,3},{3,4},{4,5},{5,6},{6,7},{7,8},{8,9},{9,10},{10,1... | collective-permute-start | bytes 393224 | tf_op jit(solution)/shard_map/ppermute | solution.py:14
  30.8 3.2 collective-permute-start.6
  35.1 3.3 copy-start.1
  35.1 3.3 copy-start.3
  38.4 15.6 %copy-start.5 = (bf16[1,64,4,128]{3,1,2,0:T(8,128)(2,1)S(1)}, bf16[1,64,4,128]{3,1,2,0:T(8,128)(2,1)}, u32[]{:S(2)}) copy-start(bf16[1,64,4,128]{3,1,2,0:T(8,128)(2,1)} %copy-done.4) | copy-start | bytes 196612
  38.4 10.9 %collective-permute-start.3 = (bf16[2,64,512]{2,1,0:T(8,128)(2,1)S(1)}, bf16[2,64,512]{2,1,0:T(8,128)(2,1)}, u32[]{:S(2)}, u32[]{:S(2)}) collective-permute-start(bf16[2,64,512]{2,1,0:T(8,128)(2,1)S(1)} %bitcast.114), channel_id=1, source_target_pairs={{1,0},{2,1},{3,2},{4,3},{5,4},{6,5},{7,6},{8,7},{9,8},{10,9},{11,1... | collective-permute-start | bytes 393224 | tf_op jit(solution)/shard_map/ppermute | solution.py:14
  39.7 8.7 %collective-permute-start.2 = (bf16[2,64,512]{2,1,0:T(8,128)(2,1)S(1)}, bf16[2,64,512]{2,1,0:T(8,128)(2,1)}, u32[]{:S(2)}, u32[]{:S(2)}) collective-permute-start(bf16[2,64,512]{2,1,0:T(8,128)(2,1)S(1)} %bitcast.115), channel_id=1, source_target_pairs={{0,1},{1,2},{2,3},{3,4},{4,5},{5,6},{6,7},{7,8},{8,9},{9,10},{10,1... | collective-permute-start | bytes 393224 | tf_op jit(solution)/shard_map/ppermute | solution.py:14
  45.8 8.2 %copy-start.7 = (bf16[1,64,4,128]{3,1,2,0:T(8,128)(2,1)S(1)}, bf16[1,64,4,128]{3,1,2,0:T(8,128)(2,1)}, u32[]{:S(2)}) copy-start(bf16[1,64,4,128]{3,1,2,0:T(8,128)(2,1)} %copy-done.6) | copy-start | bytes 196612
  48.4 5.6 %copy-start.9 = (bf16[1,64,4,128]{3,1,2,0:T(8,128)(2,1)S(1)}, bf16[1,64,4,128]{3,1,2,0:T(8,128)(2,1)}, u32[]{:S(2)}) copy-start(bf16[1,64,4,128]{3,1,2,0:T(8,128)(2,1)} %copy-done.8) | copy-start | bytes 196612
  48.4 5.6 %copy-start.11 = (bf16[1,64,4,128]{3,1,2,0:T(8,128)(2,1)S(1)}, bf16[1,64,4,128]{3,1,2,0:T(8,128)(2,1)}, u32[]{:S(2)}) copy-start(bf16[1,64,4,128]{3,1,2,0:T(8,128)(2,1)} %copy-done.10) | copy-start | bytes 196612
  53.2 0.8 copy-start.2
  57.7 4.7 %collective-permute-start.5 = (bf16[2,64,512]{2,1,0:T(8,128)(2,1)S(1)}, bf16[2,64,512]{2,1,0:T(8,128)(2,1)S(1)}, u32[]{:S(2)}, u32[]{:S(2)}) collective-permute-start(bf16[2,64,512]{2,1,0:T(8,128)(2,1)S(1)} %stack.54), channel_id=1, source_target_pairs={{0,1},{1,2},{2,3},{3,4},{4,5},{5,6},{6,7},{7,8},{8,9},{9,10},{10,1... | collective-permute-start | bytes 393224 | tf_op jit(solution)/shard_map/ppermute | solution.py:14
  60.8 4.5 %collective-permute-start.4 = (bf16[2,64,512]{2,1,0:T(8,128)(2,1)S(1)}, bf16[2,64,512]{2,1,0:T(8,128)(2,1)S(1)}, u32[]{:S(2)}, u32[]{:S(2)}) collective-permute-start(bf16[2,64,512]{2,1,0:T(8,128)(2,1)S(1)} %stack.53), channel_id=1, source_target_pairs={{1,0},{2,1},{3,2},{4,3},{5,4},{6,5},{7,6},{8,7},{9,8},{10,9},{11,1... | collective-permute-start | bytes 393224 | tf_op jit(solution)/shard_map/ppermute | solution.py:14
Sparse Core Ops, SparseCore 0:
  38.5 82.1 reduce-scatter.1
where the time goes:
time: 412 us; the launch traced here: 411 us
  blocking collectives  283 us (69%)
  waiting for transfers between devices  58.6 us (14%)
  starting transfers between devices  21.3 us (5%)
  local copies, waits for them, and re-layouts  17.3 us (4%)
  between operations  15.2 us (4%)
  matrix products  9.33 us (2%)
  other arithmetic  6.33 us (2%)
    unnamed x1, blocking collectives  283 us
    reduce_scatter x1, waiting for transfers between devices, body(): lax.psum_scatter(lax.dot_general(input_rows, grad_values, (((0,), (0,)),...  54.7 us
    ppermute x8, starting transfers between devices, from_behind(): lax.ppermute(value, axis, [(source, source + steps) for source in range(f...  21.3 us
  transfers between devices with their start and end apart: 9, of which 3 were waited for; matrix products, arithmetic and copies ran while one was open for 5% of the time, Pallas kernels for 0%

commit v1 on v0

v1 whole, which is shorter than its diff:
```python
import math

import jax
import jax.numpy as jnp
from jax import lax
from jax.experimental import pallas as pl
from jax.experimental.pallas import tpu as pltpu
from jax.sharding import Mesh, PartitionSpec as P

HD = 128
NEG = -1e30


def shift_along(value, axis, steps):
    count = lax.axis_size(axis)
    first, last = (max(0, -steps), min(count, count - steps))
    return lax.ppermute(value, axis, [(source, source + steps) for source in range(first, last)])


def contract(left, right, dims):
    return lax.dot_general(left, right, (dims, ((), ())), preferred_element_type=jnp.float32)


def attend_kernel(
    place_ref, lengths_ref, q_ref, k_ref, v_ref, g_ref, halo_lo_ref, halo_hi_ref,
    dq_ref, own_ref, halo_ref,
):
    rows = k_ref.shape[1]
    kv_heads = k_ref.shape[2] // HD
    groups = q_ref.shape[2] // HD // kv_heads
    docs = lengths_ref.shape[1]
    place = place_ref[0]
    last = place_ref[1]
    inverse_root = 1.0 / math.sqrt(HD)
    lengths = jnp.broadcast_to(lengths_ref[...], (docs, docs))
    before = lax.broadcasted_iota(jnp.int32, (docs, docs), 1) < lax.broadcasted_iota(
        jnp.int32, (docs, docs), 0
    )
    starts = jnp.sum(
        jnp.where(before, lengths, 0).astype(jnp.float32), axis=1, keepdims=True
    )
    columns = groups * rows
    for slot in range(2):
        base = place * rows if slot == 0 else (2 * last + 1 - place) * rows
        lane = lax.broadcasted_iota(jnp.int32, (docs, columns), 1)
        query_pos = (base + lax.rem(lane, rows)).astype(jnp.float32)
        first_key = jnp.max(
            jnp.where(starts <= query_pos, starts, -1.0), axis=0, keepdims=True
        )
        key_pos = (base - rows + lax.broadcasted_iota(jnp.int32, (2 * rows, columns), 0)).astype(
            jnp.float32
        )
        allowed = (key_pos >= first_key) & (key_pos <= query_pos[:1])
        for head in range(kv_heads):
            at = slice(head * HD, (head + 1) * HD)
            if slot == 0:
                key_prev, value_prev = halo_lo_ref[0, :, at], halo_lo_ref[1, :, at]
            else:
                key_prev = jnp.where(place == last, k_ref[0, :, at], halo_hi_ref[0, :, at])
                value_prev = jnp.where(place == last, v_ref[0, :, at], halo_hi_ref[1, :, at])
            key = jnp.concatenate([key_prev, k_ref[slot, :, at]], axis=0)
            value = jnp.concatenate([value_prev, v_ref[slot, :, at]], axis=0)
            wide = [
                slice((head * groups + member) * HD, (head * groups + member + 1) * HD)
                for member in range(groups)
            ]
            query = jnp.concatenate([q_ref[slot, :, one] for one in wide], axis=0)
            grad = jnp.concatenate([g_ref[slot, :, one] for one in wide], axis=0)
            scores = contract(key, query, ((1,), (1,))) * inverse_root
            scores = jnp.where(allowed, scores, NEG)
            top = jnp.max(scores, axis=0, keepdims=True)
            weight = jnp.exp(scores - top)
            probs = weight * (1.0 / jnp.sum(weight, axis=0, keepdims=True))
            probs_low = probs.astype(jnp.bfloat16)
            dprob = contract(value, grad, ((1,), (1,)))
            delta = jnp.sum(probs_low.astype(jnp.float32) * dprob, axis=0, keepdims=True)
            dscore = (probs * (dprob - delta)).astype(jnp.bfloat16)
            query_grad = (contract(dscore, key, ((0,), (0,))) * inverse_root).astype(jnp.bfloat16)
            for member, one in enumerate(wide):
                dq_ref[slot, :, one] = query_grad[member * rows : (member + 1) * rows]
            key_grad = contract(dscore, query, ((1,), (0,))) * inverse_root
            value_grad = contract(probs_low, grad, ((1,), (0,)))
            halo_ref[slot, 0, :, at] = key_grad[:rows].astype(jnp.bfloat16)
            halo_ref[slot, 1, :, at] = value_grad[:rows].astype(jnp.bfloat16)
            own_ref[slot, 0, :, at] = key_grad[rows:]
            own_ref[slot, 1, :, at] = value_grad[rows:]
            if slot == 1:
                own_ref[0, 0, :, at] += jnp.where(place == last, key_grad[:rows], 0.0)
                own_ref[0, 1, :, at] += jnp.where(place == last, value_grad[:rows], 0.0)


def attend(place, lengths, q, k, v, g, halo_lo, halo_hi):
    rows, width = k.shape[1:]
    vmem = pl.BlockSpec(memory_space=pltpu.VMEM)
    return pl.pallas_call(
        attend_kernel,
        name="attend",
        in_specs=[pl.BlockSpec(memory_space=pltpu.SMEM)] + [vmem] * 7,
        out_specs=[vmem] * 3,
        out_shape=[
            jax.ShapeDtypeStruct(q.shape, jnp.bfloat16),
            jax.ShapeDtypeStruct((2, 2, rows, width), jnp.float32),
            jax.ShapeDtypeStruct((2, 2, rows, width), jnp.bfloat16),
        ],
    )(place, lengths, q, k, v, g, halo_lo, halo_hi)


CTX = ("y", "core")


def body(queries, keys, values, out_grad, layer_input, doc_lengths):
    k, v = keys[0, 0], values[0, 0]
    ctx = lax.axis_size(CTX)
    place = jnp.stack([lax.axis_index(CTX), jnp.int32(ctx - 1)]).astype(jnp.int32)
    halo_lo = shift_along(jnp.stack([k[0], v[0]]), CTX, 1)
    halo_hi = shift_along(jnp.stack([k[1], v[1]]), CTX, -1)
    query_grad, own, halo = attend(
        place, doc_lengths, queries[0, 0], k, v, out_grad[0, 0], halo_lo, halo_hi
    )
    came = jnp.stack([shift_along(halo[0], CTX, -1), shift_along(halo[1], CTX, 1)])
    total = (own + came.astype(jnp.float32)).astype(jnp.bfloat16)
    key_grad, value_grad = total[:, 0], total[:, 1]
    tokens = 2 * k.shape[1]
    width = k.shape[2]
    depth = layer_input.shape[4]
    rows = depth // ctx
    inputs = layer_input[0, 0].reshape(tokens, ctx, rows).transpose(1, 0, 2)
    inputs = lax.all_to_all(inputs, CTX, 0, 0, tiled=True).reshape(ctx * tokens, rows)
    gathered = lax.all_gather(value_grad.reshape(tokens, width), CTX, axis=0, tiled=True)
    block = contract(gathered, inputs, ((0,), (0,)))
    for axis in ("x", "z"):
        count = lax.axis_size(axis)
        parts = block.astype(jnp.bfloat16).reshape(count, block.shape[0] // count, rows)
        parts = lax.all_to_all(parts, axis, 0, 0, tiled=True)
        block = jnp.sum(parts.astype(jnp.float32), axis=0)
    seqs = lax.axis_size(("x", "z"))
    weight_grad = block.T / jnp.float32(seqs)
    return (query_grad[None, None], key_grad[None, None], value_grad[None, None], weight_grad)


def solution(mesh):
    devices = mesh.devices
    side = math.isqrt(devices.shape[0])
    split = Mesh(devices.reshape(side, side, devices.shape[1] // 2, 2), ("x", "z", "y", "core"))
    dp, ctx = ("x", "z"), CTX
    slots = P(dp, ctx, None, None, None)
    return jax.shard_map(
        body,
        mesh=split,
        in_specs=(slots,) * 5 + (P(dp, None),),
        out_specs=(slots, slots, slots, P(ctx, dp)),
        check_vma=False,
    )
```

time: 412 us -> 144 us (0.35)
  the two profiles are of different devices: /device:TPU:8 before, /device:TPU:16 now
where the time goes in v1:
time: 144 us
  blocking collectives  69.2 us (48%)
  waiting for transfers between devices  28 us (19%)
  starting transfers between devices  18.7 us (13%)
  between operations  14.1 us (10%)
  Pallas kernels  4.88 us (3%)
  local copies, waits for them, and re-layouts  3.95 us (3%)
  other arithmetic  2.45 us (2%)
  matrix products  2.34 us (2%)
    all_to_all x2, blocking collectives, body(): parts = lax.all_to_all(parts, axis, 0, 0, tiled=True)  38.9 us
    all_to_all x1, blocking collectives, body(): lax.all_to_all(inputs, CTX, 0, 0, tiled=True).reshape(ctx * tokens, rows)  30.3 us
    all_gather x1, waiting for transfers between devices, body(): lax.all_gather(value_grad.reshape(tokens, width), CTX, axis=0, tiled=True)  21.7 us
    ppermute x4, starting transfers between devices, shift_along(): lax.ppermute(value, axis, [(source, source + steps) for source in range(f...  18.7 us
    ppermute x4, waiting for transfers between devices, shift_along(): lax.ppermute(value, axis, [(source, source + steps) for source in range(f...  6.2 us
    pallas_call x1, Pallas kernels, attend(): pl.pallas_call(attend_kernel, name='attend', in_specs=[pl.BlockSpec(memor...  4.88 us
  transfers between devices with their start and end apart: 5, of which 4 were waited for; matrix products, arithmetic and copies ran while one was open for 1% of the time, Pallas kernels for 0%

profile of v1, /device:TPU:16, one launch (start us, length us, event | category | flops | bytes accessed | tf_op | source)
XLA Modules:
  0.0 143.6 jit_solution(8525881784229688216)
XLA Ops:
  7.2 0.0 all-gather.2.cloned.1.call-start
  7.2 1.0 slice_bitcast_fusion.3
  8.2 1.9 %collective-permute-start = (bf16[2,64,512]{2,1,0:T(8,128)(2,1)S(1)}, bf16[2,64,512]{2,1,0:T(8,128)(2,1)S(1)}, u32[]{:S(2)}, u32[]{:S(2)}) collective-permute-start(bf16[2,64,512]{2,1,0:T(8,128)(2,1)S(1)} %pad_maximum_fusion), channel_id=1, source_target_pairs={{0,1},{1,2},{2,3},{3,4},{4,5},{5,6},{6,7},{7,8},{8,9},{9,10},{10,1... | collective-permute-start | bytes 393224 | tf_op jit(solution)/shard_map/ppermute | solution.py:17
  10.1 0.0 copy-start
  10.2 3.8 %collective-permute-start.1 = (bf16[2,64,512]{2,1,0:T(8,128)(2,1)S(1)}, bf16[2,64,512]{2,1,0:T(8,128)(2,1)S(1)}, u32[]{:S(2)}, u32[]{:S(2)}) collective-permute-start(bf16[2,64,512]{2,1,0:T(8,128)(2,1)S(1)} %pad_maximum_fusion.1), channel_id=1, source_target_pairs={{1,0},{2,1},{3,2},{4,3},{5,4},{6,5},{7,6},{8,7},{9,8},{10,9},{11,1... | collective-permute-start | bytes 393224 | tf_op jit(solution)/shard_map/ppermute | solution.py:17
  13.9 0.6 pad_add_fusion.place_ref
  14.6 0.0 collective-permute-done.halo_lo_ref
  14.6 0.0 copy-start.1
  14.6 1.8 %collective-permute-done.1.halo_hi_ref = bf16[2,64,512]{2,1,0:T(8,128)(2,1)S(1)} collective-permute-done((bf16[2,64,512]{2,1,0:T(8,128)(2,1)S(1)}, bf16[2,64,512]{2,1,0:T(8,128)(2,1)S(1)}, u32[]{:S(2)}, u32[]{:S(2)}) %collective-permute-start.1) | collective-permute-done | bytes 131104 | tf_op jit(solution)/shard_map/ppermute | solution.py:17
  16.4 0.0 copy-start.2
  16.4 0.0 copy-done.1
  16.4 0.7 copy-done.2
  17.1 4.9 %attend.1 = (bf16[2,64,2048]{2,1,0:T(8,128)(2,1)}, f32[2,2,64,512]{3,2,1,0:T(8,128)}, bf16[2,2,64,512]{3,2,1,0:T(8,128)(2,1)}) custom-call(s32[2]{0:T(128)} %pad_add_fusion.place_ref, s32[1,64]{1,0:T(1,128)} %lengths_ref.1, bf16[2,64,2048]{2,1,0:T(8,128)(2,1)} %bitcast.43, bf16[2,64,512]{2,1,0:T(8,128)(2,1)} %bitcast.45, bf16[2,64,512]{2,1,0:T(8,128)(2,1)} %bitcast.46, ...), custom_call_target="tpu_custom_call" | custom-call | tf_op jit(solution)/shard_map/attend/pallas_call | solution.py:95
  22.0 1.0 slice_bitcast_fusion.2
  23.0 11.1 %collective-permute-start.2 = (bf16[2,64,512]{2,1,0:T(8,128)(2,1)S(1)}, bf16[2,64,512]{2,1,0:T(8,128)(2,1)S(1)}, u32[]{:S(2)}, u32[]{:S(2)}) collective-permute-start(bf16[2,64,512]{2,1,0:T(8,128)(2,1)S(1)} %get-tuple-element.13), channel_id=1, source_target_pairs={{1,0},{2,1},{3,2},{4,3},{5,4},{6,5},{7,6},{8,7},{9,8},{10,9},{11,1... | collective-permute-start | bytes 393224 | tf_op jit(solution)/shard_map/ppermute | solution.py:17
  34.1 1.9 %collective-permute-start.3 = (bf16[2,64,512]{2,1,0:T(8,128)(2,1)S(1)}, bf16[2,64,512]{2,1,0:T(8,128)(2,1)S(1)}, u32[]{:S(2)}, u32[]{:S(2)}) collective-permute-start(bf16[2,64,512]{2,1,0:T(8,128)(2,1)S(1)} %get-tuple-element.14), channel_id=1, source_target_pairs={{0,1},{1,2},{2,3},{3,4},{4,5},{5,6},{6,7},{7,8},{8,9},{9,10},{10,1... | collective-permute-start | bytes 393224 | tf_op jit(solution)/shard_map/ppermute | solution.py:17
  36.0 0.6 collective-permute-done.2
  36.6 3.8 %collective-permute-done.3 = bf16[2,64,512]{2,1,0:T(8,128)(2,1)S(1)} collective-permute-done((bf16[2,64,512]{2,1,0:T(8,128)(2,1)S(1)}, bf16[2,64,512]{2,1,0:T(8,128)(2,1)S(1)}, u32[]{:S(2)}, u32[]{:S(2)}) %collective-permute-start.3) | collective-permute-done | bytes 131104 | tf_op jit(solution)/shard_map/ppermute | solution.py:17
  40.3 1.1 add_convert_fusion
  41.5 0.8 fusion
  42.2 0.0 all-gather.2.cloned.1.call-update
  42.3 0.0 copy-done
  42.3 0.2 copy.13
  42.5 0.3 copy.12
  42.9 30.3 %all_to_all.15 = bf16[16,128,256]{2,1,0:T(8,128)(2,1)S(1)} all-to-all(bf16[16,128,256]{2,1,0:T(8,128)(2,1)S(1)} %copy.12), channel_id=1, replica_groups=mesh['x'=8,'z'=8,'y'=8,'core'=2] {'y','core'}, dimensions={0} | all-to-all | bytes 2097152 | tf_op jit(solution)/shard_map/all_to_all | solution.py:128
  73.2 21.7 %all-gather.2.cloned.1.call-done = bf16[2048,512]{1,0:T(8,128)(2,1)} async-done(((bf16[128,512]{1,0:T(8,128)(2,1)}), bf16[2048,512]{1,0:T(8,128)(2,1)}) %all-gather.2.cloned.1.call-update) | async-done | bytes 2097168 | tf_op jit(solution)/shard_map/all_gather | solution.py:129
  94.9 2.3 %convolution_convert_fusion = bf16[512,256]{1,0:T(8,128)(2,1)S(1)} fusion(bf16[2048,512]{1,0:T(8,128)(2,1)} %all-gather.2.cloned.1.call-done, bf16[2048,256]{1,0:T(8,128)(2,1)S(1)} %bitcast.38), kind=kOutput, calls=%fused_computation | convolution fusion | flops 537001984 | bytes 3407872 | tf_op jit(solution)/shard_map/dot_general | solution.py:21
  97.2 18.7 %all_to_all.16 = bf16[8,64,256]{2,1,0:T(8,128)(2,1)S(1)} all-to-all(bf16[8,64,256]{2,1,0:T(8,128)(2,1)S(1)} %bitcast.41), channel_id=1, replica_groups=mesh['x'=8,'z'=8,'y'=8,'core'=2] {'x'}, dimensions={0} | all-to-all | bytes 524288 | tf_op jit(solution)/shard_map/all_to_all | solution.py:134
  116.0 20.1 %all_to_all.17 = bf16[8,8,256]{2,1,0:T(8,128)(2,1)S(1)} all-to-all(bf16[8,8,256]{2,1,0:T(8,128)(2,1)S(1)} %bitcast.47), channel_id=1, replica_groups=mesh['x'=8,'z'=8,'y'=8,'core'=2] {'z'}, dimensions={0} | all-to-all | bytes 65536 | tf_op jit(solution)/shard_map/all_to_all | solution.py:134
  136.2 0.6 multiply_bitcast_fusion
  (4 shorter events, 0.1 us)
Async XLA Ops:
  7.2 87.7 %all-gather.2.cloned.1.call-start = ((), (), s32[]{:S(2)}) async-start(), calls=%async_computation.3 | async-start | bytes 2228224 | tf_op jit(solution)/shard_map/all_gather | solution.py:129
  8.2 6.4 %collective-permute-start = (bf16[2,64,512]{2,1,0:T(8,128)(2,1)S(1)}, bf16[2,64,512]{2,1,0:T(8,128)(2,1)S(1)}, u32[]{:S(2)}, u32[]{:S(2)}) collective-permute-start(bf16[2,64,512]{2,1,0:T(8,128)(2,1)S(1)} %pad_maximum_fusion), channel_id=1, source_target_pairs={{0,1},{1,2},{2,3},{3,4},{4,5},{5,6},{6,7},{7,8},{8,9},{9,10},{10,1... | collective-permute-start | bytes 393224 | tf_op jit(solution)/shard_map/ppermute | solution.py:17
  10.1 32.1 %copy-start = (bf16[1,1,2,64,4096]{4,3,2,1,0:T(8,128)(2,1)S(1)}, bf16[1,1,2,64,4096]{4,3,2,1,0:T(8,128)(2,1)}, u32[]{:S(2)}) copy-start(bf16[1,1,2,64,4096]{4,3,2,1,0:T(8,128)(2,1)} %param.10) | copy-start | bytes 3145732
  10.2 6.3 %collective-permute-start.1 = (bf16[2,64,512]{2,1,0:T(8,128)(2,1)S(1)}, bf16[2,64,512]{2,1,0:T(8,128)(2,1)S(1)}, u32[]{:S(2)}, u32[]{:S(2)}) collective-permute-start(bf16[2,64,512]{2,1,0:T(8,128)(2,1)S(1)} %pad_maximum_fusion.1), channel_id=1, source_target_pairs={{1,0},{2,1},{3,2},{4,3},{5,4},{6,5},{7,6},{8,7},{9,8},{10,9},{11,1... | collective-permute-start | bytes 393224 | tf_op jit(solution)/shard_map/ppermute | solution.py:17
  14.6 1.8 %copy-start.1 = (bf16[2,64,512]{2,1,0:T(8,128)(2,1)}, bf16[2,64,512]{2,1,0:T(8,128)(2,1)S(1)}, u32[]{:S(2)}) copy-start(bf16[2,64,512]{2,1,0:T(8,128)(2,1)S(1)} %collective-permute-done.halo_lo_ref) | copy-start | bytes 393220
  16.4 0.7 copy-start.2
  23.0 13.6 %collective-permute-start.2 = (bf16[2,64,512]{2,1,0:T(8,128)(2,1)S(1)}, bf16[2,64,512]{2,1,0:T(8,128)(2,1)S(1)}, u32[]{:S(2)}, u32[]{:S(2)}) collective-permute-start(bf16[2,64,512]{2,1,0:T(8,128)(2,1)S(1)} %get-tuple-element.13), channel_id=1, source_target_pairs={{1,0},{2,1},{3,2},{4,3},{5,4},{6,5},{7,6},{8,7},{9,8},{10,9},{11,1... | collective-permute-start | bytes 393224 | tf_op jit(solution)/shard_map/ppermute | solution.py:17
  34.1 6.3 %collective-permute-start.3 = (bf16[2,64,512]{2,1,0:T(8,128)(2,1)S(1)}, bf16[2,64,512]{2,1,0:T(8,128)(2,1)S(1)}, u32[]{:S(2)}, u32[]{:S(2)}) collective-permute-start(bf16[2,64,512]{2,1,0:T(8,128)(2,1)S(1)} %get-tuple-element.14), channel_id=1, source_target_pairs={{0,1},{1,2},{2,3},{3,4},{4,5},{5,6},{6,7},{7,8},{8,9},{9,10},{10,1... | collective-permute-start | bytes 393224 | tf_op jit(solution)/shard_map/ppermute | solution.py:17
Sparse Core Ops, SparseCore 0:
  42.4 52.4 all-gather.1
